TPU v7x, 512 devices: a whole 4x8x8 slice. The times are simulated.
512 devices in a mesh: dp: 2 (over core), seq: 64 (over y, z), tensor: 4 (over x).
Axes of the slice: x: 4, y: 8, z: 8, core: 2. Of those that a mesh axis runs over, the one named last changes fastest.
Arguments:
- query: bfloat16 [2, 16384, 2048], P('dp', 'seq', 'tensor'), may hold values from -1.75 to 1.75
- key_rows: bfloat16 [2, 16384, 2048], P('dp', 'seq', 'tensor'), may hold values from -1.75 to 1.75
- value: bfloat16 [2, 16384, 2048], P('dp', 'seq', 'tensor'), may hold values from -40 to 40
- gain: float32 [2048], P('tensor'), may hold values from 0.25 to 1.75
- grad_out: bfloat16 [2, 16384, 2048], P('dp', 'seq', 'tensor'), may hold values from -16 to 16
- start_offset: int32 [2, 256], P('dp', 'seq'), may hold values from 0 to 64, as said below
Outputs:
- attn_out: bfloat16 [2, 16384, 2048], P('dp', 'seq', 'tensor')
- grad_query: bfloat16 [2, 16384, 2048], P('dp', 'seq', 'tensor')
- grad_key: bfloat16 [2, 16384, 2048], P('dp', 'seq', 'tensor')
- grad_value: bfloat16 [2, 16384, 2048], P('dp', 'seq', 'tensor')
- grad_gain: float32 [2048], P('tensor')
Inputs may be any that keep to these rules, and one draw needn't show every extreme that they name: `start_offset`: the position within its block of 64 positions at which a document starts; 64 when none starts in the block; every sequence begins a document at its first position.
All inputs are finite; a program needn't handle non-finite values.
Results may differ from a plain program's by a relative error of at most 0.0058.
Values sent between devices are 32-bit elements; how exact they have to be, the bound alone decides.
No kernel may reach another device: no remote copies, remote signals or barrier semaphores. Data moves between devices by JAX's collectives and lax.ppermute only.
A program may use at most 64 MiB of HBM per device.

v0:
```python
import jax
import jax.numpy as jnp
from jax import lax
from jax.sharding import PartitionSpec as P

DH = 128
BLK = 64
CH = 2048
eps_value = 1e-05


def carried_in(part, axis, combine, identity, reverse):
    count = lax.axis_size(axis)
    place = lax.axis_index(axis)
    ahead = count - 1 - place if reverse else place
    gathered = jax.tree.map(lambda a: lax.all_gather(a, axis), part)
    state = jax.tree.map(lambda a, e: jnp.zeros_like(a) + jnp.asarray(e, a.dtype), part, identity)

    def one(turn, state):
        source = count - 1 - turn if reverse else turn
        return combine(
            state, jax.tree.map(lambda a: lax.dynamic_index_in_dim(a, source, 0, False), gathered)
        )

    return lax.fori_loop(0, ahead, one, state)


def segment_rows(offsets, length_dev):
    positions = jnp.arange(length_dev, dtype=jnp.int32)
    block_starts = jnp.arange(offsets.shape[0], dtype=jnp.int32) * BLK + offsets
    present = offsets < BLK
    covered = (block_starts[None, :] <= positions[:, None]) & present[None, :]
    labels = jnp.sum(covered.astype(jnp.int32), axis=1)
    allowed = (labels[:, None] == labels[None, :]) & (positions[None, :] <= positions[:, None])
    starts = jnp.sum(present.astype(jnp.int32))
    return (labels, starts, allowed)


def joined(earlier, later):
    return (
        jnp.where(later[1] > 0, later[0], earlier[0] + later[0]),
        jnp.maximum(earlier[1], later[1]),
    )


def shards(query, key_rows, value, gain, grad_out, start_offset):
    length_dev = query.shape[1]
    width_local = query.shape[2]
    heads_local = width_local // DH
    query_heads = query[0].reshape(length_dev, heads_local, DH)
    key_heads = key_rows[0].reshape(length_dev, heads_local, DH)
    value_heads = value[0].reshape(length_dev, heads_local, DH)
    labels, starts, allowed = segment_rows(start_offset[0], length_dev)
    head_mask = (labels == 0)[:, None, None]
    tail_mask = (labels == starts)[:, None, None]
    reset = (starts > 0).astype(jnp.int32)
    scores = jnp.einsum("thd,shd->hts", query_heads, key_heads, preferred_element_type=jnp.float32)
    weights = jnp.where(allowed[None], scores, 0.0).astype(jnp.bfloat16)
    local_out = jnp.einsum("hts,shd->thd", weights, value_heads, preferred_element_type=jnp.float32)
    tail_keys = jnp.where(tail_mask, key_heads, jnp.zeros_like(key_heads))
    tail_values = jnp.where(tail_mask, value_heads, jnp.zeros_like(value_heads))
    tail_state = jnp.einsum(
        "shi,shj->hij", tail_keys, value_heads, preferred_element_type=jnp.float32
    )
    zero_state = jnp.zeros_like(tail_state)
    incoming = carried_in((tail_state, reset), "seq", joined, (zero_state, jnp.int32(0)), False)[0]
    carried = incoming.astype(jnp.bfloat16)
    head_query = jnp.where(head_mask, query_heads, jnp.zeros_like(query_heads))
    carried_out = jnp.einsum(
        "thi,hij->thj", head_query, carried, preferred_element_type=jnp.float32
    )
    attended = (local_out + carried_out).reshape(length_dev, width_local)
    upstream = grad_out[0].astype(jnp.float32)
    scaled = gain[None, :] * upstream
    square_local = jnp.sum(attended * attended, axis=1)
    square_total = lax.psum(square_local, "tensor")
    inverse = lax.rsqrt(square_total / CH + eps_value)
    normed = attended * inverse[:, None]
    product_total = lax.psum(jnp.sum(scaled * normed, axis=1), "tensor")
    output = (gain[None, :] * normed).astype(jnp.bfloat16)
    grad_pre = (inverse[:, None] * (scaled - normed * (product_total / CH)[:, None])).astype(
        jnp.bfloat16
    )
    gain_local = jnp.sum(upstream * normed, axis=0)
    grad_gain = lax.psum(gain_local, ("dp", "seq"))
    grad_heads = grad_pre.reshape(length_dev, heads_local, DH)
    grad_state = jnp.einsum(
        "thi,thj->hij", head_query, grad_heads, preferred_element_type=jnp.float32
    )
    later = carried_in((grad_state, reset), "seq", joined, (zero_state, jnp.int32(0)), True)[0]
    later_half = later.astype(jnp.bfloat16)
    grad_scores = jnp.einsum(
        "thd,shd->hts", grad_heads, value_heads, preferred_element_type=jnp.float32
    )
    grad_weights = jnp.where(allowed[None], grad_scores, 0.0).astype(jnp.bfloat16)
    head_grad = jnp.where(head_mask, grad_heads, jnp.zeros_like(grad_heads))
    grad_query = jnp.einsum(
        "hts,shd->thd", grad_weights, key_heads, preferred_element_type=jnp.float32
    ) + jnp.einsum("thj,hij->thi", head_grad, carried, preferred_element_type=jnp.float32)
    grad_key = jnp.einsum(
        "hts,thd->shd", grad_weights, query_heads, preferred_element_type=jnp.float32
    ) + jnp.einsum("shj,hij->shi", tail_values, later_half, preferred_element_type=jnp.float32)
    grad_value = jnp.einsum(
        "hts,thd->shd", weights, grad_heads, preferred_element_type=jnp.float32
    ) + jnp.einsum("shi,hij->shj", tail_keys, later_half, preferred_element_type=jnp.float32)
    shape_dev = (1, length_dev, width_local)
    return (
        output.reshape(shape_dev),
        grad_query.reshape(shape_dev).astype(jnp.bfloat16),
        grad_key.reshape(shape_dev).astype(jnp.bfloat16),
        grad_value.reshape(shape_dev).astype(jnp.bfloat16),
        grad_gain,
    )


def solution(mesh):
    return jax.shard_map(
        shards,
        mesh=mesh,
        in_specs=(
            P("dp", "seq", "tensor"),
            P("dp", "seq", "tensor"),
            P("dp", "seq", "tensor"),
            P("tensor"),
            P("dp", "seq", "tensor"),
            P("dp", "seq"),
        ),
        out_specs=(
            P("dp", "seq", "tensor"),
            P("dp", "seq", "tensor"),
            P("dp", "seq", "tensor"),
            P("dp", "seq", "tensor"),
            P("tensor"),
        ),
        check_vma=False,
    )
```

profile of v0, /device:TPU:1, one launch (start us, length us, event | category | flops | bytes accessed | tf_op | source)
XLA Modules:
  0.0 739.9 jit_solution(13396427716960763037)
XLA Ops:
  7.9 1.3 fusion.29
  9.2 1.1 copy.54
  10.3 1.1 copy.57
  13.8 1.1 copy.53
  14.9 1.1 copy.62
  15.9 1.3 dynamic-slice
  18.0 26.8 %all-reduce = s32[64]{0:T(128)S(1)} all-reduce(s32[64]{0:T(128)S(1)} %dynamic-update-slice), channel_id=1, replica_groups=mesh['dp'=2,'seq'=64,'tensor'=4] {'seq'}, use_global_device_ids=true, to_apply=%add | all-reduce | flops 64 | bytes 512
  45.6 112.6 %all-gather.5.cloned.1.call-done = f32[256,128,128]{2,1,0:T(8,128)} async-done(((f32[4,128,128]{2,1,0:T(8,128)}), f32[256,128,128]{2,1,0:T(8,128)}) %all-gather.5.cloned.1.call-update) | async-done | bytes 16777232 | tf_op jit(solution)/shard_map/all_gather | solution.py:16
  158.5 8.4 %psum.21 = f32[256]{0:T(256)S(1)} all-reduce(f32[256]{0:T(256)S(1)} %get-tuple-element.176), channel_id=1, replica_groups=mesh['dp'=2,'seq'=64,'tensor'=4] {'tensor'}, use_global_device_ids=true, to_apply=%region_5.6 | all-reduce | flops 256 | bytes 2048 | tf_op jit(solution)/shard_map/psum | solution.py:76
  167.1 1.2 fusion.10
  168.3 6.0 psum.22
  178.1 405.6 %psum.23 = f32[512]{0:T(512)} all-reduce(f32[512]{0:T(512)S(1)} %get-tuple-element.150), channel_id=1, replica_groups=mesh['dp'=2,'seq'=64,'tensor'=4] {'dp','seq'}, use_global_device_ids=true, to_apply=%region_11.12 | all-reduce | flops 512 | bytes 4096 | tf_op jit(solution)/shard_map/psum | solution.py:85
  585.0 145.9 %while.27 = (s32[]{:T(128)}, f32[4,128,128]{2,1,0:T(8,128)S(1)}, s32[]{:T(128)}, s32[64]{0:T(128)S(1)}, f32[64,4,128,128]{3,2,1,0:T(8,128)}, /*index=5*/s32[]{:T(128)}, s32[]{:T(128)}, s32[]{:T(128)}, s32[]{:T(128)}, s32[1]{0:T(128)}) while((s32[]{:T(128)}, f32[4,128,128]{2,1,0:T(8,128)S(1)}, s32[]{:T(128)}, s32[64]{0:T(128)S(1)}, ...), condition=%wide.region_9.10_spmd, body=%wide.region_8.9_spmd.sunk | while | flops 131079 | bytes 786613 | solution.py:25
  586.3 1.1 add_select_fusion.5
  588.6 1.1 add_select_fusion.5
  590.9 1.1 add_select_fusion.5
  595.5 1.1 add_select_fusion.5
  600.2 1.1 add_select_fusion.5
  604.8 1.1 add_select_fusion.5
  609.4 1.1 add_select_fusion.5
  614.1 1.1 add_select_fusion.5
  618.7 1.1 add_select_fusion.5
  623.3 1.1 add_select_fusion.5
  625.7 1.1 add_select_fusion.5
  (152 shorter events, 103.4 us)
Async XLA Ops:
  7.2 576.5 %copy-start = (f32[512]{0:T(512)S(1)}, f32[512]{0:T(512)}, u32[]{:S(2)}) copy-start(f32[512]{0:T(512)} %param.13) | copy-start | bytes 6148
  7.2 151.0 %all-gather.5.cloned.1.call-start = ((), (), s32[]{:S(2)}) async-start(), calls=%async_computation | async-start | bytes 17039360 | tf_op jit(solution)/shard_map/all_gather | solution.py:16
  13.1 571.9 %all-gather.7.cloned.1.call-start = ((), (), s32[]{:S(2)}) async-start(), calls=%async_computation.1 | async-start | bytes 17039360 | tf_op jit(solution)/shard_map/all_gather | solution.py:16
Sparse Core Ops, SparseCore 0:
  13.2 144.9 all-gather.4
  176.2 284.0 all-gather.6
where the time goes:
time: 743 us; the launch traced here: 740 us
  blocking collectives  447 us (60%)
  waiting for transfers between devices  113 us (15%)
  other arithmetic  71.9 us (10%)
  local copies, waits for them, and re-layouts  46.4 us (6%)
  loops' own time  42.6 us (6%)
  between operations  14.9 us (2%)
    psum x1, blocking collectives, shards(): grad_gain = lax.psum(gain_local, ('dp', 'seq'))  406 us
    all_gather x2, waiting for transfers between devices, carried_in(): gathered = jax.tree.map(lambda a: lax.all_gather(a, axis), part)  113 us
    select_n x63, other arithmetic, joined(): jnp.where(later[1] > 0, later[0], earlier[0] + later[0])  66.2 us
    another operation x2, loops' own time, carried_in(): return lax.fori_loop(0, ahead, one, state)  42.6 us
    dynamic_slice x63, local copies, waits for them, and re-layouts, one(): lax.dynamic_index_in_dim(a, source, 0, False)  37.1 us
    unnamed x1, blocking collectives  26.8 us
  transfers between devices with their start and end apart: 2, of which 1 were waited for; matrix products, arithmetic and copies ran while one was open for 1% of the time, Pallas kernels for 0%

commit v1 on v0

--- a/solution.py
+++ b/solution.py
@@ -82,7 +82,7 @@
         jnp.bfloat16
     )
     gain_local = jnp.sum(upstream * normed, axis=0)
-    grad_gain = lax.psum(gain_local, ("dp", "seq"))
+    grad_gain = lax.psum(lax.psum(gain_local, "seq"), "dp")
     grad_heads = grad_pre.reshape(length_dev, heads_local, DH)
     grad_state = jnp.einsum(
         "thi,thj->hij", head_query, grad_heads, preferred_element_type=jnp.float32

time: 743 us -> 636 us (0.86)
  blocking collectives: 447 us -> 340 us
    psum x1 -> x2, blocking collectives: 406 us -> 299 us  [shards(): grad_gain = lax.psum(lax.psum(gain_local, 'seq'), 'dp')]
where the time goes in v1:
time: 636 us; the launch traced here: 633 us
  blocking collectives  340 us (53%)
  waiting for transfers between devices  113 us (18%)
  other arithmetic  71.9 us (11%)
  local copies, waits for them, and re-layouts  46.4 us (7%)
  loops' own time  42.6 us (7%)
  between operations  14.9 us (2%)
    psum x2, blocking collectives, shards(): grad_gain = lax.psum(lax.psum(gain_local, 'seq'), 'dp')  299 us
    all_gather x2, waiting for transfers between devices, carried_in(): gathered = jax.tree.map(lambda a: lax.all_gather(a, axis), part)  113 us
    select_n x63, other arithmetic, joined(): jnp.where(later[1] > 0, later[0], earlier[0] + later[0])  66.2 us
    another operation x2, loops' own time, carried_in(): return lax.fori_loop(0, ahead, one, state)  42.6 us
    dynamic_slice x63, local copies, waits for them, and re-layouts, one(): lax.dynamic_index_in_dim(a, source, 0, False)  37.1 us
    unnamed x1, blocking collectives  26.8 us
  transfers between devices with their start and end apart: 2, of which 1 were waited for; matrix products, arithmetic and copies ran while one was open for 1% of the time, Pallas kernels for 0%

profile of v1, /device:TPU:1, one launch (start us, length us, event | category | flops | bytes accessed | tf_op | source)
XLA Modules:
  0.0 633.0 jit_solution(306783847588512424)
XLA Ops:
  7.9 1.3 fusion.29
  9.2 1.1 copy.54
  10.3 1.1 copy.57
  13.8 1.1 copy.53
  14.9 1.1 copy.62
  15.9 1.3 dynamic-slice
  18.0 26.8 %all-reduce = s32[64]{0:T(128)S(1)} all-reduce(s32[64]{0:T(128)S(1)} %dynamic-update-slice), channel_id=1, replica_groups=mesh['dp'=2,'seq'=64,'tensor'=4] {'seq'}, use_global_device_ids=true, to_apply=%add | all-reduce | flops 64 | bytes 512
  45.6 112.6 %all-gather.5.cloned.1.call-done = f32[256,128,128]{2,1,0:T(8,128)} async-done(((f32[4,128,128]{2,1,0:T(8,128)}), f32[256,128,128]{2,1,0:T(8,128)}) %all-gather.5.cloned.1.call-update) | async-done | bytes 16777232 | tf_op jit(solution)/shard_map/all_gather | solution.py:16
  158.5 8.4 %psum.28 = f32[256]{0:T(256)S(1)} all-reduce(f32[256]{0:T(256)S(1)} %get-tuple-element.176), channel_id=1, replica_groups=mesh['dp'=2,'seq'=64,'tensor'=4] {'tensor'}, use_global_device_ids=true, to_apply=%region_5.6 | all-reduce | flops 256 | bytes 2048 | tf_op jit(solution)/shard_map/psum | solution.py:76
  167.1 1.2 fusion.10
  168.3 6.0 psum.29
  178.1 263.6 %psum.30 = f32[512]{0:T(512)S(1)} all-reduce(f32[512]{0:T(512)S(1)} %get-tuple-element.150), channel_id=1, replica_groups=mesh['dp'=2,'seq'=64,'tensor'=4] {'seq'}, use_global_device_ids=true, to_apply=%region_11.12 | all-reduce | flops 512 | bytes 4096 | tf_op jit(solution)/shard_map/psum | solution.py:85
  441.6 35.1 %psum.31 = f32[512]{0:T(512)} all-reduce(f32[512]{0:T(512)S(1)} %psum.30), channel_id=1, replica_groups=mesh['dp'=2,'seq'=64,'tensor'=4] {'dp'}, use_global_device_ids=true, to_apply=%region_12.13 | all-reduce | flops 512 | bytes 4096 | tf_op jit(solution)/shard_map/psum | solution.py:85
  478.0 145.9 %while.27 = (s32[]{:T(128)}, f32[4,128,128]{2,1,0:T(8,128)S(1)}, s32[]{:T(128)}, s32[64]{0:T(128)S(1)}, f32[64,4,128,128]{3,2,1,0:T(8,128)}, /*index=5*/s32[]{:T(128)}, s32[]{:T(128)}, s32[]{:T(128)}, s32[]{:T(128)}, s32[1]{0:T(128)}) while((s32[]{:T(128)}, f32[4,128,128]{2,1,0:T(8,128)S(1)}, s32[]{:T(128)}, s32[64]{0:T(128)S(1)}, ...), condition=%wide.region_9.10_spmd, body=%wide.region_8.9_spmd.sunk | while | flops 131079 | bytes 786613 | solution.py:25
  481.6 1.1 add_select_fusion.5
  486.3 1.1 add_select_fusion.5
  490.9 1.1 add_select_fusion.5
  495.5 1.1 add_select_fusion.5
  497.8 1.1 add_select_fusion.5
  500.2 1.1 add_select_fusion.5
  502.5 1.1 add_select_fusion.5
  504.8 1.1 add_select_fusion.5
  507.1 1.1 add_select_fusion.5
  511.7 1.1 add_select_fusion.5
  (153 shorter events, 104.5 us)
Async XLA Ops:
  7.2 469.5 %copy-start = (f32[512]{0:T(512)S(1)}, f32[512]{0:T(512)}, u32[]{:S(2)}) copy-start(f32[512]{0:T(512)} %param.13) | copy-start | bytes 6148
  7.2 151.0 %all-gather.5.cloned.1.call-start = ((), (), s32[]{:S(2)}) async-start(), calls=%async_computation | async-start | bytes 17039360 | tf_op jit(solution)/shard_map/all_gather | solution.py:16
  13.1 465.0 %all-gather.7.cloned.1.call-start = ((), (), s32[]{:S(2)}) async-start(), calls=%async_computation.1 | async-start | bytes 17039360 | tf_op jit(solution)/shard_map/all_gather | solution.py:16
Sparse Core Ops, SparseCore 0:
  13.2 144.9 all-gather.4
  176.2 283.9 all-gather.6
